TPU v7x, 32 devices: a whole 2x2x4 slice. The times are simulated.
32 devices in a mesh: req: 8 (over z, y), tp: 4 (over x, core).
Axes of the slice: x: 2, y: 2, z: 4, core: 2. Of those that a mesh axis runs over, the one named last changes fastest.
Arguments:
- residual: bfloat16 [256, 2048], P('req'), may hold values from -6 to 6
- cache_lengths: int32 [256], P('req'), may hold values from 4 to 4096, as said below
- input_gain: float32 [2048], replicated, may hold values from 0.1 to 1.9
- inner_weight: bfloat16 [2048, 2, 1536], P(None, None, 'tp'), may hold values from -0.125 to 0.125
- step_weight: bfloat16 [2048, 24], P(None, 'tp'), may hold values from -0.125 to 0.125
- step_bias: float32 [24], P('tp'), may hold values from -4 to -1
- decay_log: float32 [24], P('tp'), may hold values from 0 to 2.77
- skip_gain: float32 [24], P('tp'), may hold values from 0.5 to 2
- conv_weight: bfloat16 [4, 1536], P(None, 'tp'), may hold values from -3 to 3
- conv_state: bfloat16 [256, 3, 1536], P('req', None, 'tp'), may hold values from -6 to 6
- coupling_weight: bfloat16 [2048, 512], P(None, 'tp'), may hold values from -0.125 to 0.125
- coupling_conv: bfloat16 [4, 512], P(None, 'tp'), may hold values from -3 to 3
- coupling_state: bfloat16 [256, 3, 512], P('req', None, 'tp'), may hold values from -6 to 6
- scan_state: bfloat16 [256, 24, 64, 256], P('req', 'tp'), may hold values from -30 to 30
- mixer_gain: float32 [1536], P('tp'), may hold values from 0.1 to 1.9
- attention_weight: bfloat16 [2048, 1536], P(None, 'tp'), may hold values from -0.125 to 0.125
- sink_cache: bfloat16 [256, 4, 512], P('req'), may hold values from -2000 to 2000
- window_cache: bfloat16 [256, 1024, 512], P('req', 'tp'), may hold values from -9 to 9
- mamba_out: bfloat16 [1536, 2048], P('tp'), may hold values from -0.15625 to 0.15625
- attention_out: bfloat16 [1024, 2048], P('tp'), may hold values from -0.5 to 0.5
- final_gain: float32 [2048], replicated, may hold values from 0.1 to 1.9
- output_head: bfloat16 [2048, 65536], P(None, ('req', 'tp')), may hold values from -0.375 to 0.375
Outputs:
- new_residual: bfloat16 [256, 2048], P('req', 'tp')
- logits: float32 [256, 65536], P(('req', 'tp'))
- new_scan_state: bfloat16 [256, 24, 64, 256], P('req', 'tp')
- new_conv_state: bfloat16 [256, 3, 1536], P('req', None, 'tp')
- new_coupling_state: bfloat16 [256, 3, 512], P('req', None, 'tp')
- new_key_value: bfloat16 [256, 512], P('req')
Inputs may be any that keep to these rules, and one draw needn't show every extreme that they name: `cache_lengths`: A request's cache holds positions 0 to its length - 1; the new token stands at the position equal to the length. Some request has length exactly 4096.
All inputs are finite; a program needn't handle non-finite values.
Results may differ from a plain program's by a relative error of at most 0.02.
Values may be sent and summed in bfloat16 or wider, within the bound.
A program may use at most 128 MiB of HBM per device.

v0:
```python
import jax
import jax.numpy as jnp
from jax import lax
from jax.sharding import PartitionSpec as P

MH = 24
MP = 64
NS = 256
QH = 8
KVH = 2
HD = 128
WIN = 1024
SINK = 4
EPSILON = 1e-05
NEG_BIG = -1e30


def combined_all(array, axis, combine):
    everything = jax.tree.map(
        lambda part, kind: lax.all_gather(part.astype(kind), axis),
        array,
        (jnp.bfloat16, jnp.bfloat16, jnp.bfloat16),
    )

    def take(k):
        return jax.tree.map(lambda part, own: part[k].astype(own.dtype), everything, array)

    return lax.fori_loop(
        1, lax.axis_size(axis), lambda k, so_far: combine(so_far, take(k)), take(0)
    )


def norm_rows(values, gain):
    widened = values.astype(jnp.float32)
    mean_sq = jnp.mean(widened * widened, axis=-1, keepdims=True)
    return (widened * lax.rsqrt(mean_sq + EPSILON) * gain).astype(jnp.bfloat16)


def conv_apply(old_state, fresh_row, taps):
    window = jnp.concatenate([old_state, fresh_row[:, None, :]], axis=1)
    mixed_rows = jnp.einsum("rkc,kc->rc", window, taps, preferred_element_type=jnp.float32)
    return (jax.nn.silu(mixed_rows), window[:, 1:, :])


def merge_parts(first_part, second_part):
    first_peak, first_total, first_sum = first_part
    second_peak, second_total, second_sum = second_part
    row_peak = jnp.maximum(first_peak, second_peak)
    first_scale = jnp.exp(first_peak - row_peak)
    second_scale = jnp.exp(second_peak - row_peak)
    return (
        row_peak,
        first_total * first_scale + second_total * second_scale,
        first_sum * first_scale[..., None] + second_sum * second_scale[..., None],
    )


def attend_part(queries, key_rows, value_rows, valid_mask):
    scores = jnp.einsum(
        "rkgd,rskd->rkgs", queries, key_rows, preferred_element_type=jnp.float32
    ) * HD ** (-0.5)
    masked = jnp.where(valid_mask, scores, NEG_BIG)
    row_peak = jnp.max(masked, axis=-1)
    weights = jnp.where(valid_mask, jnp.exp(masked - row_peak[..., None]), 0.0)
    totals = jnp.sum(weights, axis=-1)
    summed = jnp.einsum(
        "rkgs,rskd->rkgd",
        weights.astype(jnp.bfloat16),
        value_rows,
        preferred_element_type=jnp.float32,
    )
    return (row_peak, totals, summed)


def body(
    residual,
    cache_lengths,
    input_gain,
    inner_weight,
    step_weight,
    step_bias,
    decay_log,
    skip_gain,
    conv_weight,
    conv_state,
    coupling_weight,
    coupling_conv,
    coupling_state,
    scan_state,
    mixer_gain,
    attention_weight,
    sink_cache,
    window_cache,
    mamba_out,
    attention_out,
    final_gain,
    output_head,
):
    row_count = residual.shape[0]
    tp_size = lax.axis_size("tp")
    tp_index = lax.axis_index("tp")
    local_heads = scan_state.shape[1]
    local_units = inner_weight.shape[2]
    half_width = KVH * HD
    group_size = QH // KVH
    normed = norm_rows(residual, input_gain)
    projected = jnp.einsum(
        "rd,dtc->rtc", normed, inner_weight, preferred_element_type=jnp.float32
    ).astype(jnp.bfloat16)
    gate_rows = lax.optimization_barrier(projected[:, 0, :])
    x_rows, new_conv_state = conv_apply(conv_state, projected[:, 1, :], conv_weight)
    step_rows = lax.optimization_barrier(
        jnp.dot(normed, step_weight, preferred_element_type=jnp.float32).astype(jnp.bfloat16)
    )
    step_size = jax.nn.softplus(step_rows.astype(jnp.float32) + step_bias)
    decay_rate = jnp.exp(-step_size * jnp.exp(decay_log))
    coupling_pre = jnp.dot(normed, coupling_weight, preferred_element_type=jnp.float32).astype(
        jnp.bfloat16
    )
    coupling_rows, new_coupling_state = conv_apply(coupling_state, coupling_pre, coupling_conv)
    qkv_local = jnp.dot(normed, attention_weight, preferred_element_type=jnp.float32).astype(
        jnp.bfloat16
    )
    qkv_rows, coupling_all = (
        lax.all_gather(qkv_local, "tp", axis=1, tiled=True),
        lax.all_gather(coupling_rows.astype(jnp.bfloat16), "tp", axis=1, tiled=True),
    )
    input_vec = coupling_all[:, :NS].astype(jnp.float32)
    output_vec = coupling_all[:, NS:].astype(jnp.float32)
    x_heads = x_rows.reshape(row_count, local_heads, MP)
    updated = (
        decay_rate[:, :, None, None] * scan_state.astype(jnp.float32)
        + (step_size[:, :, None] * x_heads)[:, :, :, None] * input_vec[:, None, None, :]
    )
    readout = (
        jnp.einsum("rhpn,rn->rhp", updated, output_vec, precision=lax.Precision.HIGHEST)
        + skip_gain[None, :, None] * x_heads
    )
    new_scan_state = updated.astype(jnp.bfloat16)
    gated_rows = readout.reshape(row_count, local_units) * jax.nn.silu(
        gate_rows.astype(jnp.float32)
    )
    square_total = lax.psum(jnp.sum(gated_rows * gated_rows, axis=1), "tp")
    mamba_rows = (
        gated_rows * lax.rsqrt(square_total / (MH * MP) + EPSILON)[:, None] * mixer_gain
    ).astype(jnp.bfloat16)
    queries = qkv_rows[:, : QH * HD].reshape(row_count, KVH, group_size, HD)
    fresh_keys = qkv_rows[:, QH * HD : QH * HD + half_width].reshape(row_count, 1, KVH, HD)
    fresh_values = qkv_rows[:, QH * HD + half_width :].reshape(row_count, 1, KVH, HD)
    new_key_value = qkv_rows[:, QH * HD :]
    is_lead = tp_index == 0
    sink_keys = sink_cache[:, :, :half_width].reshape(row_count, SINK, KVH, HD)
    sink_values = sink_cache[:, :, half_width:].reshape(row_count, SINK, KVH, HD)
    sink_part = attend_part(
        queries, sink_keys, sink_values, jnp.broadcast_to(is_lead, (row_count, 1, 1, SINK))
    )
    fresh_part = attend_part(
        queries, fresh_keys, fresh_values, jnp.broadcast_to(is_lead, (row_count, 1, 1, 1))
    )
    window_slots = window_cache.shape[1]
    slot_offset = tp_index * window_slots
    length_column = cache_lengths[:, None]
    cycle_keys = window_cache[:, :, :half_width].reshape(row_count, window_slots, KVH, HD)
    cycle_values = window_cache[:, :, half_width:].reshape(row_count, window_slots, KVH, HD)
    slot_index = slot_offset + jnp.arange(window_slots, dtype=jnp.int32)
    back_steps = (length_column - 1 - slot_index[None, :]) % WIN
    position = length_column - 1 - back_steps
    live_mask = ((position >= SINK) & (back_steps != WIN - 1))[:, None, None, :]
    cycle_part = attend_part(queries, cycle_keys, cycle_values, live_mask)
    local_peak, local_total, local_sum = merge_parts(merge_parts(sink_part, fresh_part), cycle_part)
    row_peak, totals, summed = combined_all((local_peak, local_total, local_sum), "tp", merge_parts)
    attended = (summed / totals[..., None]).reshape(row_count, QH * HD).astype(jnp.bfloat16)
    head_columns = QH // tp_size * HD
    own_heads = lax.dynamic_slice_in_dim(attended, tp_index * head_columns, head_columns, 1)
    mixed_rows = jnp.dot(mamba_rows, mamba_out, preferred_element_type=jnp.float32) + jnp.dot(
        own_heads, attention_out, preferred_element_type=jnp.float32
    )
    share_width = residual.shape[1] // tp_size
    mixed_total = lax.psum(mixed_rows.astype(jnp.bfloat16), "tp").astype(jnp.float32)
    new_full = (residual.astype(jnp.float32) + mixed_total).astype(jnp.bfloat16)
    new_residual = lax.dynamic_slice_in_dim(new_full, tp_index * share_width, share_width, 1)
    final_rows = norm_rows(new_full, final_gain)
    vocab_logits = jnp.dot(
        lax.all_gather(final_rows, "req", axis=0, tiled=True),
        output_head,
        preferred_element_type=jnp.float32,
    )
    logits = lax.all_to_all(
        vocab_logits.astype(jnp.bfloat16), ("req", "tp"), split_axis=0, concat_axis=1, tiled=True
    ).astype(vocab_logits.dtype)
    return (new_residual, logits, new_scan_state, new_conv_state, new_coupling_state, new_key_value)


def solution(mesh):
    return jax.shard_map(
        body,
        mesh=mesh,
        in_specs=(
            P("req", None),
            P("req"),
            P(),
            P(None, None, "tp"),
            P(None, "tp"),
            P("tp"),
            P("tp"),
            P("tp"),
            P(None, "tp"),
            P("req", None, "tp"),
            P(None, "tp"),
            P(None, "tp"),
            P("req", None, "tp"),
            P("req", "tp", None, None),
            P("tp"),
            P(None, "tp"),
            P("req", None, None),
            P("req", "tp", None),
            P("tp", None),
            P("tp", None),
            P(),
            P(None, ("req", "tp")),
        ),
        out_specs=(
            P("req", "tp"),
            P(("req", "tp"), None),
            P("req", "tp", None, None),
            P("req", None, "tp"),
            P("req", None, "tp"),
            P("req", None),
        ),
        check_vma=False,
    )
```

profile of v0, /device:TPU:0, one launch (start us, length us, event | category | flops | bytes accessed | tf_op | source)
XLA Modules:
  0.0 261.5 jit_solution(11709163570320856122)
XLA Ops:
  7.2 1.2 fusion.24
  8.4 1.9 convolution_convert_fusion.1
  10.3 6.3 %all_gather.24 = bf16[32,1536]{1,0:T(8,128)(2,1)S(1)} all-gather(bf16[32,384]{1,0:T(8,128)(2,1)S(1)} %convolution_convert_fusion.1), channel_id=1, replica_groups=mesh['req'=8,'tp'=4] {'tp'}, dimensions={1}, use_global_device_ids=true | all-gather | bytes 122880 | tf_op jit(solution)/shard_map/all_gather | solution.py:125
  18.6 6.0 %fusion.79 = (bf16[32,256,256]{2,1,0:T(8,128)(2,1)}, bf16[32,256,256]{2,1,0:T(8,128)(2,1)}) fusion(bf16[32,256,512]{2,1,0:T(8,128)(2,1)} %param.41), kind=kLoop, calls=%fused_computation.140 | loop fusion | bytes 16777216 | tf_op jit(solution)/shard_map/slice | solution.py:164
  24.6 6.5 %copy.137 = bf16[32,256,256]{1,2,0:T(8,128)(2,1)} copy(bf16[32,256,256]{2,1,0:T(8,128)(2,1)} %get-tuple-element.233) | data formatting | bytes 8388608
  31.2 2.9 %fusion.80 = (f32[32,2,4]{2,1,0:T(2,128)S(1)}, f32[32,2,4,256]{3,2,1,0:T(4,128)S(1)}) fusion(bf16[32,2,4,128]{3,2,1,0:T(4,128)(2,1)S(1)} %reshape.220, bf16[32,256,2,128]{1,3,2,0:T(8,128)(2,1)} %bitcast.108, pred[32,256]{1,0:T(8,128)(4,1)S(1)} %fusion.52), kind=kOutput, calls=%fused_computation.141 | convolution fusion | flops 16973568 | bytes 4531200 | tf_op jit(solution)/shard_map/rkgd,rskd->rkgs/dot_general | solution.py:59
  34.9 0.9 fusion.29
  35.8 1.4 copy.96
  37.2 1.7 fusion.38
  38.9 1.0 copy.84
  39.9 1.3 reshape.257
  41.3 1.6 fusion.81
  42.8 0.8 copy.128
  44.3 1.3 max.53
  45.6 1.3 add_convert_fusion
  49.7 0.8 copy.98
  51.2 1.4 copy.105
  52.6 6.5 %copy.138 = bf16[32,256,256]{1,2,0:T(8,128)(2,1)} copy(bf16[32,256,256]{2,1,0:T(8,128)(2,1)} %get-tuple-element.232) | data formatting | bytes 8388608
  59.1 1.4 fusion.15
  60.5 0.8 copy-done.1
  61.4 2.2 fusion.16
  63.6 6.4 %all-gather.2 = bf16[128,2,4,128]{3,2,1,0:T(4,128)(2,1)S(1)} all-gather(bf16[32,2,4,128]{3,2,1,0:T(4,128)(2,1)S(1)} %fusion.16), channel_id=4, replica_groups=mesh['req'=8,'tp'=4] {'tp'}, dimensions={0}, use_global_device_ids=true | all-gather | bytes 327680 | tf_op jit(solution)/shard_map/all_gather | solution.py:20
  70.7 0.7 copy.97
  71.4 5.4 %all-gather.1 = bf16[128,2,4]{2,1,0:T(2,128)(2,1)S(1)} all-gather(bf16[32,2,4]{2,1,0:T(2,128)(2,1)} %copy.97), channel_id=3, replica_groups=mesh['req'=8,'tp'=4] {'tp'}, dimensions={0}, use_global_device_ids=true | all-gather | bytes 2560 | tf_op jit(solution)/shard_map/all_gather | solution.py:20
  77.4 0.8 copy.109
  78.3 0.7 copy.111
  79.0 1.4 copy.90
  80.4 5.4 %all-gather = bf16[128,2,4]{2,1,0:T(2,128)(2,1)S(1)} all-gather(bf16[32,2,4]{2,1,0:T(2,128)(2,1)} %copy.90), channel_id=2, replica_groups=mesh['req'=8,'tp'=4] {'tp'}, dimensions={0}, use_global_device_ids=true | all-gather | bytes 2560 | tf_op jit(solution)/shard_map/all_gather | solution.py:20
  86.5 1.4 copy.108
  87.9 0.7 copy.110
  88.6 8.4 %while.19 = (s32[]{:T(128)}, f32[32,2,4]{0,2,1:T(4,128)}, f32[32,2,4]{0,2,1:T(4,128)S(1)}, f32[32,2,4,128]{3,2,1,0:T(4,128)S(1)}, bf16[4,32,2,4]{1,3,2,0:T(4,128...) while((s32[]{:T(128)}, f32[32,2,4]{0,2,1:T(4,128)}, ...), condition=%wide.region_8.9_spmd, body=%wide.region_7.8_spmd.sunk | while | flops 133125 | bytes 341143 | solution.py:28
  88.6 1.3 fusion.98
  90.1 1.3 fusion.99
  91.4 1.3 fusion.98
  92.9 1.3 fusion.99
  94.2 1.3 fusion.98
  95.7 1.3 fusion.99
  97.0 0.7 copy.112
  97.7 0.9 divide_convert_fusion
  99.3 1.4 fusion.17
  102.1 0.9 reshape.218
  103.0 1.0 convolution_convert_fusion.3
  104.6 0.7 multiply_exponential_fusion
  106.1 1.3 fusion.20
  108.1 0.7 multiply_reduce_fusion.1
  108.9 5.2 %all_gather.23 = bf16[32,512]{1,0:T(8,128)(2,1)S(1)} all-gather(bf16[32,128]{1,0:T(8,128)(2,1)S(1)} %fusion.61), channel_id=1, replica_groups=mesh['req'=8,'tp'=4] {'tp'}, dimensions={1}, use_global_device_ids=true | all-gather | bytes 40960 | tf_op jit(solution)/shard_map/all_gather | solution.py:126
  115.3 0.8 broadcast_multiply_fusion
  116.2 10.6 %fusion.4 = f32[32,1,6,64]{3,1,2,0:T(1,128)S(1)} fusion(bf16[32,6,64,256]{3,2,1,0:T(8,128)(2,1)} %param.37, f32[32,256]{1,0:T(8,128)} %get-tuple-element.239, f32[32,6,64]{2,1,0:T(8,128)S(1)} %broadcast_multiply_fusion, f32[32,6]{1,0:T(8,128)} %copy.81, bf16[32,256,1,1]{1,0,2,3:T(8,128)(2,1)} %get-tuple-element.238), kind=kOutput, calls=%fused_computation.10 | convolution fusion | flops 50331648 | bytes 6439680 | tf_op jit(solution)/shard_map/rhpn,rn->rhp/dot_general | solution.py:136
  126.8 0.7 bitcast_add_fusion
  127.5 1.0 reshape.219
  128.7 7.4 %psum.14 = f32[32]{0:T(128)S(1)} all-reduce(f32[32]{0:T(128)S(1)} %multiply_reduce_fusion.2), channel_id=1, replica_groups=mesh['req'=8,'tp'=4] {'tp'}, use_global_device_ids=true, to_apply=%region_2.3 | all-reduce | flops 32 | bytes 256 | tf_op jit(solution)/shard_map/psum | solution.py:143
  136.1 1.8 fusion.54
  137.9 2.2 fusion.11
  140.2 31.8 %all-reduce.2.cloned.1.call-done = bf16[32,2048]{1,0:T(8,128)(2,1)} async-done(((bf16[32,2048]{1,0:T(8,128)(2,1)}), bf16[32,2048]{1,0:T(8,128)(2,1)}) %all-reduce.2.cloned.1.call-update) | async-done | bytes 131088 | tf_op jit(solution)/shard_map/psum | solution.py:179
  172.0 1.1 fusion.21
  173.1 0.8 fusion.23
  173.9 41.2 %all-gather.5.cloned.1.call-done = bf16[256,2048]{1,0:T(8,128)(2,1)} async-done(((bf16[32,2048]{1,0:T(8,128)(2,1)}), bf16[256,2048]{1,0:T(8,128)(2,1)}) %all-gather.5.cloned.1.call-update) | async-done | bytes 1048592 | tf_op jit(solution)/shard_map/all_gather | solution.py:184
  215.1 7.0 %fusion.10 = bf16[32,8,2048]{2,1,0:T(8,128)(2,1)} fusion(bf16[256,2048]{1,0:T(8,128)(2,1)} %all-gather.5.cloned.1.call-done, bf16[2048,2048]{1,0:T(8,128)(2,1)} %param.45), kind=kOutput, calls=%fused_computation.17 | convolution fusion | flops 2148007936 | bytes 10485760 | tf_op jit(solution)/shard_map/dot_general | solution.py:183
  222.1 3.5 %all-to-all-start = ((bf16[32,8,2048]{2,1,0:T(8,128)(2,1)}), bf16[32,8,2048]{2,1,0:T(8,128)(2,1)}, u32[]{:S(2)}, u32[]{:S(2)}) async-start(bf16[32,8,2048]{2,1,0:T(8,128)(2,1)} %fusion.10), calls=%async_computation | async-start | bytes 2097152 | tf_op jit(solution)/shard_map/all_to_all | solution.py:188
  225.6 1.4 slice.85
  227.0 1.3 fusion.53
  229.0 8.1 %fusion.3 = bf16[32,6,64,256]{3,2,1,0:T(8,128)(2,1)} fusion(bf16[32,6,64,256]{3,2,1,0:T(8,128)(2,1)} %param.37, f32[32,256]{1,0:T(8,128)S(1)} %copy-done.11, f32[32,6,64]{2,1,0:T(8,128)S(1)} %copy-done.7, f32[32,6]{1,0:T(8,128)} %copy.81), kind=kLoop, calls=%fused_computation.9 | loop fusion | flops 15728640 | bytes 12665600 | tf_op jit(solution)/shard_map/convert_element_type | solution.py:139
  237.7 14.2 %all-to-all-done = bf16[32,8,2048]{2,1,0:T(8,128)(2,1)} async-done(((bf16[32,8,2048]{2,1,0:T(8,128)(2,1)}), bf16[32,8,2048]{2,1,0:T(8,128)(2,1)}, u32[]{:S(2)}, u32[]{:S(2)}) %all-to-all-start) | async-done | bytes 1048608 | tf_op jit(solution)/shard_map/all_to_all | solution.py:188
  251.8 2.8 %convert_element_type.203 = f32[32,8,2048]{2,1,0:T(8,128)} convert(bf16[32,8,2048]{2,1,0:T(8,128)(2,1)} %all-to-all-done) | non-fusion elementwise | flops 524288 | bytes 3145728 | tf_op jit(solution)/shard_map/convert_element_type | solution.py:190
  (90 shorter events, 16.5 us)
Async XLA Ops:
  7.2 92.1 %copy-start = (bf16[2048,2,384]{2,1,0:T(2,128)(2,1)S(1)}, bf16[2048,2,384]{2,1,0:T(2,128)(2,1)}, u32[]{:S(2)}) copy-start(bf16[2048,2,384]{2,1,0:T(2,128)(2,1)} %param.27) | copy-start | bytes 9437188
  7.2 164.8 %all-reduce.2.cloned.1.call-start = ((), (), s32[]{:S(2)}) async-start(), calls=%async_computation.1 | async-start | bytes 262144 | tf_op jit(solution)/shard_map/psum | solution.py:179
  8.4 8.2 %copy-start.20 = (f32[32]{0:T(128)}, f32[32]{0:T(128)S(1)}, u32[]{:S(2)}) copy-start(f32[32]{0:T(128)S(1)} %add_rsqrt_fusion.2) | copy-start | bytes 388
  16.6 0.7 copy-start.5
  31.2 6.0 %copy-start.14 = (pred[32,256]{1,0:T(8,128)(4,1)}, pred[32,256]{1,0:T(8,128)(4,1)S(1)}, u32[]{:S(2)}) copy-start(pred[32,256]{1,0:T(8,128)(4,1)S(1)} %fusion.52) | copy-start | bytes 24580
  34.2 24.9 %copy-start.4 = (f32[32,2,4,256]{3,2,1,0:T(4,128)}, f32[32,2,4,256]{3,2,1,0:T(4,128)S(1)}, u32[]{:S(2)}) copy-start(f32[32,2,4,256]{3,2,1,0:T(4,128)S(1)} %get-tuple-element.246) | copy-start | bytes 786436
  51.2 7.9 %copy-start.16 = (f32[32,2,4]{2,1,0:T(2,128)S(1)}, f32[32,2,4]{2,1,0:T(2,128)}, u32[]{:S(2)}) copy-start(f32[32,2,4]{2,1,0:T(2,128)} %copy.100) | copy-start | bytes 3076
  52.6 7.9 %copy-start.15 = (pred[32,256]{1,0:T(8,128)(4,1)S(1)}, pred[32,256]{1,0:T(8,128)(4,1)}, u32[]{:S(2)}) copy-start(pred[32,256]{1,0:T(8,128)(4,1)} %copy-done.14) | copy-start | bytes 24580
  59.1 2.3 copy-start.1
  59.1 2.3 copy-start.17
  59.1 11.5 %copy-start.19 = (bf16[32,2,4]{0,2,1:T(4,128)(2,1)S(1)}, bf16[32,2,4]{0,2,1:T(4,128)(2,1)}, u32[]{:S(2)}) copy-start(bf16[32,2,4]{0,2,1:T(4,128)(2,1)} %get-tuple-element.228) | copy-start | bytes 1540
  60.5 38.8 %copy-start.2 = (bf16[32,2048]{1,0:T(8,128)(2,1)S(1)}, bf16[32,2048]{1,0:T(8,128)(2,1)}, u32[]{:S(2)}) copy-start(bf16[32,2048]{1,0:T(8,128)(2,1)} %param.24) | copy-start | bytes 393220
  63.6 37.8 %copy-start.8 = (bf16[32,3,384]{2,0,1:T(8,128)(2,1)S(1)}, bf16[32,3,384]{2,0,1:T(8,128)(2,1)}, u32[]{:S(2)}) copy-start(bf16[32,3,384]{2,0,1:T(8,128)(2,1)} %param.33) | copy-start | bytes 221188
  69.9 0.7 copy-start.3
  100.7 26.1 %copy-start.9 = (bf16[32,1,384]{2,0,1:T(8,128)(2,1)}, bf16[32,1,384]{2,0,1:T(8,128)(2,1)S(1)}, u32[]{:S(2)}) copy-start(bf16[32,1,384]{2,0,1:T(8,128)(2,1)S(1)} %get-tuple-element.237) | copy-start | bytes 73732
  107.4 19.4 %copy-start.12 = (bf16[32,1,128]{2,0,1:T(8,128)(2,1)}, bf16[32,1,128]{2,0,1:T(8,128)(2,1)S(1)}, u32[]{:S(2)}) copy-start(bf16[32,1,128]{2,0,1:T(8,128)(2,1)S(1)} %fusion.20) | copy-start | bytes 24580
  116.2 10.6 %copy-start.6 = (f32[32,6,64]{2,1,0:T(8,128)}, f32[32,6,64]{2,1,0:T(8,128)S(1)}, u32[]{:S(2)}) copy-start(f32[32,6,64]{2,1,0:T(8,128)S(1)} %broadcast_multiply_fusion) | copy-start | bytes 147460
  116.2 10.6 %copy-start.22 = (f32[6]{0:T(128)S(1)}, f32[6]{0:T(128)}, u32[]{:S(2)}) copy-start(f32[6]{0:T(128)} %param.31) | copy-start | bytes 76
  116.2 19.9 %copy-start.21 = (f32[384]{0:T(512)S(1)}, f32[384]{0:T(512)}, u32[]{:S(2)}) copy-start(f32[384]{0:T(512)} %param.38) | copy-start | bytes 4612
  116.2 56.9 %copy-start.18 = (f32[2048]{0:T(1024)S(1)}, f32[2048]{0:T(1024)}, u32[]{:S(2)}) copy-start(f32[2048]{0:T(1024)} %param.44) | copy-start | bytes 24580
  140.1 75.0 %all-gather.5.cloned.1.call-start = ((), (), s32[]{:S(2)}) async-start(), calls=%async_computation.2 | async-start | bytes 1179648 | tf_op jit(solution)/shard_map/all_gather | solution.py:184
  173.9 53.1 %copy-start.13 = (bf16[32,1,128]{2,0,1:T(8,128)(2,1)S(1)}, bf16[32,1,128]{2,0,1:T(8,128)(2,1)}, u32[]{:S(2)}) copy-start(bf16[32,1,128]{2,0,1:T(8,128)(2,1)} %copy-done.12) | copy-start | bytes 24580
  173.9 54.5 %copy-start.10 = (bf16[32,1,384]{2,0,1:T(8,128)(2,1)S(1)}, bf16[32,1,384]{2,0,1:T(8,128)(2,1)}, u32[]{:S(2)}) copy-start(bf16[32,1,384]{2,0,1:T(8,128)(2,1)} %copy-done.9) | copy-start | bytes 73732
  173.9 55.1 %copy-start.7 = (f32[32,6,64]{2,1,0:T(8,128)S(1)}, f32[32,6,64]{2,1,0:T(8,128)}, u32[]{:S(2)}) copy-start(f32[32,6,64]{2,1,0:T(8,128)} %copy-done.6) | copy-start | bytes 147460
  173.9 55.1 %copy-start.11 = (f32[32,256]{1,0:T(8,128)S(1)}, f32[32,256]{1,0:T(8,128)}, u32[]{:S(2)}) copy-start(f32[32,256]{1,0:T(8,128)} %get-tuple-element.239) | copy-start | bytes 98308
  222.1 29.7 %all-to-all-start = ((bf16[32,8,2048]{2,1,0:T(8,128)(2,1)}), bf16[32,8,2048]{2,1,0:T(8,128)(2,1)}, u32[]{:S(2)}, u32[]{:S(2)}) async-start(bf16[32,8,2048]{2,1,0:T(8,128)(2,1)} %fusion.10), calls=%async_computation | async-start | bytes 2097152 | tf_op jit(solution)/shard_map/all_to_all | solution.py:188
Sparse Core Ops, SparseCore 0:
  140.2 31.7 all-reduce.1
  174.9 40.1 all-gather.4
where the time goes:
time: 264 us; the launch traced here: 261 us
  waiting for transfers between devices  87.2 us (33%)
  local copies, waits for them, and re-layouts  46.1 us (17%)
  other arithmetic  37.1 us (14%)
  matrix products  37 us (14%)
  blocking collectives  36.1 us (14%)
  between operations  14.4 us (5%)
  starting transfers between devices  3.56 us (1%)
    all_gather x1, waiting for transfers between devices, body(): lax.all_gather(final_rows, 'req', axis=0, tiled=True)  41.2 us
    psum x1, waiting for transfers between devices, body(): lax.psum(mixed_rows.astype(jnp.bfloat16), 'tp').astype(jnp.float32)  31.8 us
    all_gather x3, blocking collectives, combined_all(): lax.all_gather(part.astype(kind), axis)  17.2 us
    unnamed x48, local copies, waits for them, and re-layouts  15.3 us
    all_to_all x1, waiting for transfers between devices, body(): lax.all_to_all(vocab_logits.astype(jnp.bfloat16), ('req', 'tp'), split_ax...  14.2 us
    dot_general x1, matrix products, body(): jnp.einsum('rhpn,rn->rhp', updated, output_vec, precision=lax.Precision.H...  10.6 us
    convert_element_type x1, other arithmetic, body(): new_scan_state = updated.astype(jnp.bfloat16)  8.08 us
    psum x1, blocking collectives, body(): square_total = lax.psum(jnp.sum(gated_rows * gated_rows, axis=1), 'tp')  7.38 us
  transfers between devices with their start and end apart: 3, of which 3 were waited for; matrix products, arithmetic and copies ran while one was open for 5% of the time, Pallas kernels for 0%

commit v1 on v0

--- a/solution.py
+++ b/solution.py
@@ -2,6 +2,7 @@
 import jax.numpy as jnp
 from jax import lax
 from jax.sharding import PartitionSpec as P
+from jax.lax import all_to_all, axis_size
 
 MH = 24
 MP = 64
@@ -13,6 +14,17 @@
 SINK = 4
 EPSILON = 1e-05
 NEG_BIG = -1e30
+
+
+def _order_members_all(block_in):
+    finding = all_to_all(
+        jnp.stack(jnp.split(block_in, axis_size(("req", "tp")), axis=0)),
+        ("req", "tp"),
+        split_axis=0,
+        concat_axis=0,
+    )
+    carry_out = jnp.concatenate(finding, axis=1)
+    return carry_out
 
 
 def combined_all(array, axis, combine):
@@ -185,9 +197,7 @@
         output_head,
         preferred_element_type=jnp.float32,
     )
-    logits = lax.all_to_all(
-        vocab_logits.astype(jnp.bfloat16), ("req", "tp"), split_axis=0, concat_axis=1, tiled=True
-    ).astype(vocab_logits.dtype)
+    logits = _order_members_all(vocab_logits.astype(jnp.bfloat16)).astype(vocab_logits.dtype)
     return (new_residual, logits, new_scan_state, new_conv_state, new_coupling_state, new_key_value)
 
 

time: 264 us -> 283 us (1.072)
  local copies, waits for them, and re-layouts: 46.1 us -> 65.8 us
    unnamed x48 -> x79, local copies, waits for them, and re-layouts: 15.3 us -> 34.4 us
  transfers between devices with their start and end apart: 3 -> 3, of which waited for: 3 -> 3; matrix products, arithmetic and copies ran while one was open for 5% -> 4% of each run, Pallas kernels for 0% -> 0%
where the time goes in v1:
time: 283 us; the launch traced here: 280 us
  waiting for transfers between devices  87.2 us (31%)
  local copies, waits for them, and re-layouts  65.8 us (23%)
  other arithmetic  37.1 us (13%)
  blocking collectives  36.1 us (13%)
  matrix products  36 us (13%)
  between operations  14.4 us (5%)
  starting transfers between devices  3.56 us (1%)
    all_gather x1, waiting for transfers between devices, body(): lax.all_gather(final_rows, 'req', axis=0, tiled=True)  41.2 us
    unnamed x79, local copies, waits for them, and re-layouts  34.4 us
    psum x1, waiting for transfers between devices, body(): lax.psum(mixed_rows.astype(jnp.bfloat16), 'tp').astype(jnp.float32)  31.8 us
    all_gather x3, blocking collectives, combined_all(): lax.all_gather(part.astype(kind), axis)  17.2 us
    all_to_all x1, waiting for transfers between devices, _order_members_all(): all_to_all(jnp.stack(jnp.split(block_in, axis_size(('req', 'tp')), axis=0...  14.2 us
    dot_general x1, matrix products, body(): jnp.einsum('rhpn,rn->rhp', updated, output_vec, precision=lax.Precision.H...  10.6 us
    convert_element_type x1, other arithmetic, body(): new_scan_state = updated.astype(jnp.bfloat16)  8.08 us
    psum x1, blocking collectives, body(): square_total = lax.psum(jnp.sum(gated_rows * gated_rows, axis=1), 'tp')  7.38 us
  transfers between devices with their start and end apart: 3, of which 3 were waited for; matrix products, arithmetic and copies ran while one was open for 4% of the time, Pallas kernels for 0%

profile of v1, /device:TPU:0, one launch (start us, length us, event | category | flops | bytes accessed | tf_op | source)
XLA Modules:
  0.0 280.2 jit_solution(2752281246695487277)
XLA Ops:
  7.2 1.2 fusion.23
  8.4 1.9 convolution_convert_fusion.1
  10.3 6.3 %all_gather.24 = bf16[32,1536]{1,0:T(8,128)(2,1)S(1)} all-gather(bf16[32,384]{1,0:T(8,128)(2,1)S(1)} %convolution_convert_fusion.1), channel_id=1, replica_groups=mesh['req'=8,'tp'=4] {'tp'}, dimensions={1}, use_global_device_ids=true | all-gather | bytes 122880 | tf_op jit(solution)/shard_map/all_gather | solution.py:137
  18.6 6.0 %fusion.78 = (bf16[32,256,256]{2,1,0:T(8,128)(2,1)}, bf16[32,256,256]{2,1,0:T(8,128)(2,1)}) fusion(bf16[32,256,512]{2,1,0:T(8,128)(2,1)} %param.41), kind=kLoop, calls=%fused_computation.203 | loop fusion | bytes 16777216 | tf_op jit(solution)/shard_map/slice | solution.py:176
  24.6 6.5 %copy.137 = bf16[32,256,256]{1,2,0:T(8,128)(2,1)} copy(bf16[32,256,256]{2,1,0:T(8,128)(2,1)} %get-tuple-element.233) | data formatting | bytes 8388608
  31.2 2.9 %fusion.79 = (f32[32,2,4]{2,1,0:T(2,128)S(1)}, f32[32,2,4,256]{3,2,1,0:T(4,128)S(1)}) fusion(bf16[32,2,4,128]{3,2,1,0:T(4,128)(2,1)S(1)} %reshape.219, bf16[32,256,2,128]{1,3,2,0:T(8,128)(2,1)} %bitcast.234, pred[32,256]{1,0:T(8,128)(4,1)S(1)} %fusion.51), kind=kOutput, calls=%fused_computation.204 | convolution fusion | flops 16973568 | bytes 4531200 | tf_op jit(solution)/shard_map/rkgd,rskd->rkgs/dot_general | solution.py:71
  34.9 0.9 fusion.28
  35.8 1.4 copy.96
  37.2 1.7 fusion.37
  38.9 1.0 copy.84
  39.9 1.3 reshape.256
  41.3 1.6 fusion.80
  42.8 0.8 copy.128
  44.3 1.3 max.53
  45.6 1.3 add_convert_fusion
  49.7 0.8 copy.98
  51.2 1.4 copy.105
  52.6 6.5 %copy.138 = bf16[32,256,256]{1,2,0:T(8,128)(2,1)} copy(bf16[32,256,256]{2,1,0:T(8,128)(2,1)} %get-tuple-element.232) | data formatting | bytes 8388608
  59.1 1.4 fusion.14
  60.5 0.8 copy-done.1
  61.4 2.2 fusion.15
  63.6 6.4 %all-gather.2 = bf16[128,2,4,128]{3,2,1,0:T(4,128)(2,1)S(1)} all-gather(bf16[32,2,4,128]{3,2,1,0:T(4,128)(2,1)S(1)} %fusion.15), channel_id=4, replica_groups=mesh['req'=8,'tp'=4] {'tp'}, dimensions={0}, use_global_device_ids=true | all-gather | bytes 327680 | tf_op jit(solution)/shard_map/all_gather | solution.py:32
  70.7 0.7 copy.97
  71.4 5.4 %all-gather.1 = bf16[128,2,4]{2,1,0:T(2,128)(2,1)S(1)} all-gather(bf16[32,2,4]{2,1,0:T(2,128)(2,1)} %copy.97), channel_id=3, replica_groups=mesh['req'=8,'tp'=4] {'tp'}, dimensions={0}, use_global_device_ids=true | all-gather | bytes 2560 | tf_op jit(solution)/shard_map/all_gather | solution.py:32
  77.4 0.8 copy.109
  78.3 0.7 copy.111
  79.0 1.4 copy.90
  80.4 5.4 %all-gather = bf16[128,2,4]{2,1,0:T(2,128)(2,1)S(1)} all-gather(bf16[32,2,4]{2,1,0:T(2,128)(2,1)} %copy.90), channel_id=2, replica_groups=mesh['req'=8,'tp'=4] {'tp'}, dimensions={0}, use_global_device_ids=true | all-gather | bytes 2560 | tf_op jit(solution)/shard_map/all_gather | solution.py:32
  86.5 1.4 copy.108
  87.9 0.7 copy.110
  88.6 8.4 %while.19 = (s32[]{:T(128)}, f32[32,2,4]{0,2,1:T(4,128)}, f32[32,2,4]{0,2,1:T(4,128)S(1)}, f32[32,2,4,128]{3,2,1,0:T(4,128)S(1)}, bf16[4,32,2,4]{1,3,2,0:T(4,128...) while((s32[]{:T(128)}, f32[32,2,4]{0,2,1:T(4,128)}, ...), condition=%wide.region_8.9_spmd, body=%wide.region_7.8_spmd.sunk | while | flops 133125 | bytes 341143 | solution.py:40
  88.6 1.3 fusion.97
  90.1 1.3 fusion.98
  91.4 1.3 fusion.97
  92.9 1.3 fusion.98
  94.2 1.3 fusion.97
  95.7 1.3 fusion.98
  97.0 0.7 copy.112
  97.7 0.9 divide_convert_fusion
  99.3 1.4 fusion.16
  102.1 0.9 reshape.217
  103.0 1.0 convolution_convert_fusion.3
  104.6 0.7 multiply_exponential_fusion
  106.1 1.3 fusion.19
  108.1 0.7 multiply_reduce_fusion.1
  108.9 5.2 %all_gather.23 = bf16[32,512]{1,0:T(8,128)(2,1)S(1)} all-gather(bf16[32,128]{1,0:T(8,128)(2,1)S(1)} %fusion.60), channel_id=1, replica_groups=mesh['req'=8,'tp'=4] {'tp'}, dimensions={1}, use_global_device_ids=true | all-gather | bytes 40960 | tf_op jit(solution)/shard_map/all_gather | solution.py:138
  115.3 0.8 broadcast_multiply_fusion
  116.2 10.6 %fusion.4 = f32[32,1,6,64]{3,1,2,0:T(1,128)S(1)} fusion(bf16[32,6,64,256]{3,2,1,0:T(8,128)(2,1)} %param.37, f32[32,256]{1,0:T(8,128)} %get-tuple-element.239, f32[32,6,64]{2,1,0:T(8,128)S(1)} %broadcast_multiply_fusion, f32[32,6]{1,0:T(8,128)} %copy.81, bf16[32,256,1,1]{1,0,2,3:T(8,128)(2,1)} %get-tuple-element.238), kind=kOutput, calls=%fused_computation.10 | convolution fusion | flops 50331648 | bytes 6439680 | tf_op jit(solution)/shard_map/rhpn,rn->rhp/dot_general | solution.py:148
  126.8 0.7 bitcast_add_fusion
  127.5 1.0 reshape.218
  128.7 7.4 %psum.14 = f32[32]{0:T(128)S(1)} all-reduce(f32[32]{0:T(128)S(1)} %multiply_reduce_fusion.2), channel_id=1, replica_groups=mesh['req'=8,'tp'=4] {'tp'}, use_global_device_ids=true, to_apply=%region_2.3 | all-reduce | flops 32 | bytes 256 | tf_op jit(solution)/shard_map/psum | solution.py:155
  136.1 1.8 fusion.53
  137.9 2.2 fusion.10
  140.2 31.8 %all-reduce.2.cloned.1.call-done = bf16[32,2048]{1,0:T(8,128)(2,1)} async-done(((bf16[32,2048]{1,0:T(8,128)(2,1)}), bf16[32,2048]{1,0:T(8,128)(2,1)}) %all-reduce.2.cloned.1.call-update) | async-done | bytes 131088 | tf_op jit(solution)/shard_map/psum | solution.py:191
  172.0 1.1 fusion.20
  173.1 0.8 fusion.22
  173.9 41.2 %all-gather.5.cloned.1.call-done = bf16[256,2048]{1,0:T(8,128)(2,1)} async-done(((bf16[32,2048]{1,0:T(8,128)(2,1)}), bf16[256,2048]{1,0:T(8,128)(2,1)}) %all-gather.5.cloned.1.call-update) | async-done | bytes 1048592 | tf_op jit(solution)/shard_map/all_gather | solution.py:196
  215.1 6.0 %convolution_convert_fusion = bf16[256,2048]{1,0:T(8,128)(2,1)S(1)} fusion(bf16[256,2048]{1,0:T(8,128)(2,1)} %all-gather.5.cloned.1.call-done, bf16[2048,2048]{1,0:T(8,128)(2,1)} %param.45), kind=kOutput, calls=%fused_computation.16 | convolution fusion | flops 2148007936 | bytes 10485760 | tf_op jit(solution)/shard_map/dot_general | solution.py:195
  240.9 3.5 %all-to-all-start = ((bf16[32,8,2048]{2,1,0:T(8,128)(2,1)}), bf16[32,8,2048]{2,1,0:T(8,128)(2,1)}, u32[]{:S(2)}, u32[]{:S(2)}) async-start(bf16[32,8,2048]{2,1,0:T(8,128)(2,1)} %constant_dynamic-update-slice_fusion), calls=%async_computation | async-start | bytes 2097152 | tf_op jit(solution)/shard_map/all_to_all | solution.py:20
  244.4 1.4 slice.85
  245.8 1.3 fusion.52
  247.8 8.1 %fusion.3 = bf16[32,6,64,256]{3,2,1,0:T(8,128)(2,1)} fusion(bf16[32,6,64,256]{3,2,1,0:T(8,128)(2,1)} %param.37, f32[32,256]{1,0:T(8,128)S(1)} %copy-done.11, f32[32,6,64]{2,1,0:T(8,128)S(1)} %copy-done.7, f32[32,6]{1,0:T(8,128)} %copy.81), kind=kLoop, calls=%fused_computation.9 | loop fusion | flops 15728640 | bytes 12665600 | tf_op jit(solution)/shard_map/convert_element_type | solution.py:151
  256.5 14.2 %all-to-all-done = bf16[32,8,2048]{2,1,0:T(8,128)(2,1)} async-done(((bf16[32,8,2048]{2,1,0:T(8,128)(2,1)}), bf16[32,8,2048]{2,1,0:T(8,128)(2,1)}, u32[]{:S(2)}, u32[]{:S(2)}) %all-to-all-start) | async-done | bytes 1048608 | tf_op jit(solution)/shard_map/all_to_all | solution.py:20
  270.6 2.8 convert_element_type.203
  (122 shorter events, 36.2 us)
Async XLA Ops:
  7.2 92.1 %copy-start = (bf16[2048,2,384]{2,1,0:T(2,128)(2,1)S(1)}, bf16[2048,2,384]{2,1,0:T(2,128)(2,1)}, u32[]{:S(2)}) copy-start(bf16[2048,2,384]{2,1,0:T(2,128)(2,1)} %param.27) | copy-start | bytes 9437188
  7.2 164.8 %all-reduce.2.cloned.1.call-start = ((), (), s32[]{:S(2)}) async-start(), calls=%async_computation.1 | async-start | bytes 262144 | tf_op jit(solution)/shard_map/psum | solution.py:191
  8.4 8.2 %copy-start.20 = (f32[32]{0:T(128)}, f32[32]{0:T(128)S(1)}, u32[]{:S(2)}) copy-start(f32[32]{0:T(128)S(1)} %add_rsqrt_fusion.2) | copy-start | bytes 388
  16.6 0.7 copy-start.5
  31.2 6.0 %copy-start.14 = (pred[32,256]{1,0:T(8,128)(4,1)}, pred[32,256]{1,0:T(8,128)(4,1)S(1)}, u32[]{:S(2)}) copy-start(pred[32,256]{1,0:T(8,128)(4,1)S(1)} %fusion.51) | copy-start | bytes 24580
  34.2 24.9 %copy-start.4 = (f32[32,2,4,256]{3,2,1,0:T(4,128)}, f32[32,2,4,256]{3,2,1,0:T(4,128)S(1)}, u32[]{:S(2)}) copy-start(f32[32,2,4,256]{3,2,1,0:T(4,128)S(1)} %get-tuple-element.246) | copy-start | bytes 786436
  51.2 7.9 %copy-start.16 = (f32[32,2,4]{2,1,0:T(2,128)S(1)}, f32[32,2,4]{2,1,0:T(2,128)}, u32[]{:S(2)}) copy-start(f32[32,2,4]{2,1,0:T(2,128)} %copy.100) | copy-start | bytes 3076
  52.6 7.9 %copy-start.15 = (pred[32,256]{1,0:T(8,128)(4,1)S(1)}, pred[32,256]{1,0:T(8,128)(4,1)}, u32[]{:S(2)}) copy-start(pred[32,256]{1,0:T(8,128)(4,1)} %copy-done.14) | copy-start | bytes 24580
  59.1 2.3 copy-start.1
  59.1 2.3 copy-start.17
  59.1 11.5 %copy-start.19 = (bf16[32,2,4]{0,2,1:T(4,128)(2,1)S(1)}, bf16[32,2,4]{0,2,1:T(4,128)(2,1)}, u32[]{:S(2)}) copy-start(bf16[32,2,4]{0,2,1:T(4,128)(2,1)} %get-tuple-element.228) | copy-start | bytes 1540
  60.5 38.8 %copy-start.2 = (bf16[32,2048]{1,0:T(8,128)(2,1)S(1)}, bf16[32,2048]{1,0:T(8,128)(2,1)}, u32[]{:S(2)}) copy-start(bf16[32,2048]{1,0:T(8,128)(2,1)} %param.24) | copy-start | bytes 393220
  63.6 37.8 %copy-start.8 = (bf16[32,3,384]{2,0,1:T(8,128)(2,1)S(1)}, bf16[32,3,384]{2,0,1:T(8,128)(2,1)}, u32[]{:S(2)}) copy-start(bf16[32,3,384]{2,0,1:T(8,128)(2,1)} %param.33) | copy-start | bytes 221188
  69.9 0.7 copy-start.3
  100.7 26.1 %copy-start.9 = (bf16[32,1,384]{2,0,1:T(8,128)(2,1)}, bf16[32,1,384]{2,0,1:T(8,128)(2,1)S(1)}, u32[]{:S(2)}) copy-start(bf16[32,1,384]{2,0,1:T(8,128)(2,1)S(1)} %get-tuple-element.237) | copy-start | bytes 73732
  107.4 19.4 %copy-start.12 = (bf16[32,1,128]{2,0,1:T(8,128)(2,1)}, bf16[32,1,128]{2,0,1:T(8,128)(2,1)S(1)}, u32[]{:S(2)}) copy-start(bf16[32,1,128]{2,0,1:T(8,128)(2,1)S(1)} %fusion.19) | copy-start | bytes 24580
  116.2 10.6 %copy-start.6 = (f32[32,6,64]{2,1,0:T(8,128)}, f32[32,6,64]{2,1,0:T(8,128)S(1)}, u32[]{:S(2)}) copy-start(f32[32,6,64]{2,1,0:T(8,128)S(1)} %broadcast_multiply_fusion) | copy-start | bytes 147460
  116.2 10.6 %copy-start.22 = (f32[6]{0:T(128)S(1)}, f32[6]{0:T(128)}, u32[]{:S(2)}) copy-start(f32[6]{0:T(128)} %param.31) | copy-start | bytes 76
  116.2 19.9 %copy-start.21 = (f32[384]{0:T(512)S(1)}, f32[384]{0:T(512)}, u32[]{:S(2)}) copy-start(f32[384]{0:T(512)} %param.38) | copy-start | bytes 4612
  116.2 56.9 %copy-start.18 = (f32[2048]{0:T(1024)S(1)}, f32[2048]{0:T(1024)}, u32[]{:S(2)}) copy-start(f32[2048]{0:T(1024)} %param.44) | copy-start | bytes 24580
  140.1 75.0 %all-gather.5.cloned.1.call-start = ((), (), s32[]{:S(2)}) async-start(), calls=%async_computation.2 | async-start | bytes 1179648 | tf_op jit(solution)/shard_map/all_gather | solution.py:196
  173.9 71.9 %copy-start.13 = (bf16[32,1,128]{2,0,1:T(8,128)(2,1)S(1)}, bf16[32,1,128]{2,0,1:T(8,128)(2,1)}, u32[]{:S(2)}) copy-start(bf16[32,1,128]{2,0,1:T(8,128)(2,1)} %copy-done.12) | copy-start | bytes 24580
  173.9 73.2 %copy-start.10 = (bf16[32,1,384]{2,0,1:T(8,128)(2,1)S(1)}, bf16[32,1,384]{2,0,1:T(8,128)(2,1)}, u32[]{:S(2)}) copy-start(bf16[32,1,384]{2,0,1:T(8,128)(2,1)} %copy-done.9) | copy-start | bytes 73732
  173.9 73.9 %copy-start.7 = (f32[32,6,64]{2,1,0:T(8,128)S(1)}, f32[32,6,64]{2,1,0:T(8,128)}, u32[]{:S(2)}) copy-start(f32[32,6,64]{2,1,0:T(8,128)} %copy-done.6) | copy-start | bytes 147460
  173.9 73.9 %copy-start.11 = (f32[32,256]{1,0:T(8,128)S(1)}, f32[32,256]{1,0:T(8,128)}, u32[]{:S(2)}) copy-start(f32[32,256]{1,0:T(8,128)} %get-tuple-element.239) | copy-start | bytes 98308
  240.9 29.7 %all-to-all-start = ((bf16[32,8,2048]{2,1,0:T(8,128)(2,1)}), bf16[32,8,2048]{2,1,0:T(8,128)(2,1)}, u32[]{:S(2)}, u32[]{:S(2)}) async-start(bf16[32,8,2048]{2,1,0:T(8,128)(2,1)} %constant_dynamic-update-slice_fusion), calls=%async_computation | async-start | bytes 2097152 | tf_op jit(solution)/shard_map/all_to_all | solution.py:20
Sparse Core Ops, SparseCore 0:
  140.2 31.7 all-reduce.1
  174.9 40.1 all-gather.4
